TPU v7x, 256 devices: a whole 4x4x8 slice. The times are simulated.
256 devices in a mesh: req: 16 (over x_hi, y, core), ctx: 16 (over x_lo, z).
Axes of the slice: x: 4 (x_hi: 2, x_lo: 2; x = x_hi * 2 + x_lo), y: 4, z: 8, core: 2. Of those that a mesh axis runs over, the one named last changes fastest.
Arguments:
- queries: bfloat16 [1024, 8192], P(('req', 'ctx')), parts along dimension 0, may hold values from -15 to 15
- new_keys: bfloat16 [1024, 512], P(('req', 'ctx')), parts along dimension 0, may hold values from -9 to 9
- new_values: bfloat16 [1024, 512], P(('req', 'ctx')), parts along dimension 0, may hold values from -6 to 6
- cache_keys: bfloat16 [524288, 512], P(('req', 'ctx')), parts along dimension 0, may hold values from -6 to 6
- cache_values: bfloat16 [524288, 512], P(('req', 'ctx')), parts along dimension 0, may hold values from -6 to 6
- cache_length: int32 [16], P('req'), parts along dimension 0, may hold values from 8192 to 32767
- page_table: int32 [4096], P('req'), parts along dimension 0, may hold values from 0 to 255, each once
Outputs:
- attended: bfloat16 [1024, 8192], P(('req', 'ctx')), parts along dimension 0
There are 16 independent parts, one for each index of `req`. A program takes and returns all parts, laid end to end along the dimension named above; each array names one. Nothing has to cross between parts.
Inputs may be any that keep to these rules, and one draw needn't show every extreme that they name: A permutation: logical page p lies in physical rows page_table[p] * 128 to page_table[p] * 128 + 127.
All inputs are finite; a program needn't handle non-finite values.
Results may differ from a plain program's by a relative error of at most 0.004.
Values may be sent and summed in bfloat16 or wider, within the bound.
No kernel may reach another device: no remote copies, remote signals or barrier semaphores. Data moves between devices by JAX's collectives and lax.ppermute only.
A program may use at most 64 MiB of HBM per device.

v0:
```python
import jax
import jax.numpy as jnp
from jax import lax
from jax.sharding import PartitionSpec as P

KVH = 4
HD = 128
PAGE = 128
floor_score = -1e30


def from_behind(x, axis, by):
    devices = lax.axis_size(axis)
    return lax.ppermute(x, axis, [(i, (i + by) % devices) for i in range(devices)])


def attend(queries, query_pos, keys, values, key_pos, key_ok):
    rows = queries.shape[0]
    heads = queries.shape[1] // HD
    grouped = queries.reshape(rows, KVH, heads // KVH, HD)
    key_count = keys.shape[0]
    keys_grouped = keys.reshape(key_count, KVH, HD)
    values_grouped = values.reshape(key_count, KVH, HD)
    scores = jnp.einsum(
        "rkgd,nkd->rkgn", grouped, keys_grouped, preferred_element_type=jnp.float32
    ) * HD ** (-0.5)
    allowed = key_ok[None, :] & (key_pos[None, :] <= query_pos[:, None])
    allowed = allowed[:, None, None, :]
    scores = jnp.where(allowed, scores, floor_score)
    top = jnp.max(scores, axis=3)
    weights = jnp.where(allowed, jnp.exp(scores - top[..., None]), 0.0)
    total = jnp.sum(weights, axis=3)
    mixed = jnp.einsum(
        "rkgn,nkd->rkgd",
        weights.astype(jnp.bfloat16),
        values_grouped,
        preferred_element_type=jnp.float32,
    )
    return (mixed.reshape(rows, heads * HD), top.reshape(rows, heads), total.reshape(rows, heads))


def combine(first, second):
    mixed_first, top_first, total_first = first
    mixed_second, top_second, total_second = second
    rows, heads = top_first.shape
    top = jnp.maximum(top_first, top_second)
    factor_first = jnp.exp(top_first - top)
    factor_second = jnp.exp(top_second - top)
    mixed = (
        mixed_first.reshape(rows, heads, HD) * factor_first[..., None]
        + mixed_second.reshape(rows, heads, HD) * factor_second[..., None]
    )
    return (
        mixed.reshape(rows, heads * HD),
        top,
        factor_first * total_first + factor_second * total_second,
    )


def empty_state(rows, heads):
    return (
        jnp.zeros((rows, heads * HD), jnp.float32),
        jnp.full((rows, heads), floor_score, jnp.float32),
        jnp.zeros((rows, heads), jnp.float32),
    )


def settle(moved):
    return (moved[0], moved[1], moved[2], moved[3])


def local(queries, new_keys, new_values, cache_keys, cache_values, cache_length, page_table):
    count = lax.axis_size("ctx")
    device = lax.axis_index("ctx")
    rows = queries.shape[0]
    heads = queries.shape[1] // HD
    local_pages = cache_keys.shape[0] // PAGE
    length = cache_length[0]
    slots = device * local_pages + lax.iota(jnp.int32, local_pages)
    hits = (page_table[:, None] == slots[None, :]).astype(jnp.int32)
    logical = jnp.sum(hits * lax.iota(jnp.int32, page_table.shape[0])[:, None], axis=0)
    cache_pos = (logical[:, None] * PAGE + lax.iota(jnp.int32, PAGE)[None, :]).reshape(-1)
    cache_live = cache_pos < length
    own_pos = length + device * rows + lax.iota(jnp.int32, rows)

    def attend_cache(held, positions):
        return attend(held, positions, cache_keys, cache_values, cache_pos, cache_live)

    keys_piece = lax.all_gather(new_keys, "ctx", axis=0, tiled=True)
    values_piece = lax.all_gather(new_values, "ctx", axis=0, tiled=True)
    piece_rows = keys_piece.shape[0]
    key_pos = length + lax.iota(jnp.int32, piece_rows)
    span_state = combine(
        empty_state(rows, heads),
        attend(queries, own_pos, keys_piece, values_piece, key_pos, jnp.ones((piece_rows,), bool)),
    )

    def hop_one(step, carry):
        held = carry[0]
        source = (device - step) % count
        positions = length + source * rows + lax.iota(jnp.int32, rows)
        state = combine(carry[1:4], attend_cache(held, positions))
        return settle(from_behind((held,) + state, "ctx", 1))

    final = lax.fori_loop(0, count, hop_one, (queries,) + empty_state(rows, heads))
    cycle_state = final[1:4]
    mixed, top, total = combine(cycle_state, span_state)
    result = mixed.reshape(rows, heads, HD) / total[..., None]
    return result.reshape(rows, heads * HD).astype(jnp.bfloat16)


def solution(mesh):
    in_specs = (
        P(("req", "ctx"), None),
        P(("req", "ctx"), None),
        P(("req", "ctx"), None),
        P(("req", "ctx"), None),
        P(("req", "ctx"), None),
        P("req"),
        P("req"),
    )
    out_specs = P(("req", "ctx"), None)
    return jax.shard_map(local, mesh=mesh, in_specs=in_specs, out_specs=out_specs, check_vma=False)
```

profile of v0, /device:TPU:2, one launch (start us, length us, event | category | flops | bytes accessed | tf_op | source)
XLA Modules:
  0.0 324.2 jit_solution(2116719299812118511)
XLA Ops:
  2.5 35.9 %all-gather = bf16[16,4,512]{2,1,0:T(4,128)(2,1)S(1)} all-gather(bf16[1,4,512]{2,1,0:T(4,128)(2,1)} %bitcast.139), channel_id=1, replica_groups=mesh['req'=16,'ctx'=16] {'ctx'}, dimensions={0}, use_global_device_ids=true | all-gather | bytes 69632 | tf_op jit(solution)/shard_map/all_gather | solution.py:89
  38.4 30.2 %all-gather.1 = bf16[16,4,512]{2,1,0:T(4,128)(2,1)S(1)} all-gather(bf16[1,4,512]{2,1,0:T(4,128)(2,1)} %bitcast.140), channel_id=1, replica_groups=mesh['req'=16,'ctx'=16] {'ctx'}, dimensions={0}, use_global_device_ids=true | all-gather | bytes 69632 | tf_op jit(solution)/shard_map/all_gather | solution.py:90
  69.5 4.1 %reshape.248 = bf16[2048,4,128]{2,1,0:T(4,128)(2,1)} reshape(bf16[2048,512]{1,0:T(8,128)(2,1)} %param.12) | data formatting | bytes 4194304 | tf_op jit(solution)/shard_map/while/body/eval_jaxpr/reshape | solution.py:22
  73.7 2.0 reshape.249
  75.7 247.0 %while.24 = (s32[]{:T(128)}, bf16[4,8192]{1,0:T(4,128)(2,1)S(1)}, f32[4,8192]{1,0:T(4,128)S(1)}, f32[4,64]{1,0:T(4,128)S(1)}, f32[4,64]{1,0:T(4,128)S(1)}, /*ind...) while((s32[]{:T(128)}, bf16[4,8192]{1,0:T(4,128)(2,1)S(1)}, ...), condition=%wide.wide.region_4.5_spmd.clone.clone, body=%wide.wide.region_1.4_spmd.clone.clone.sunk | while | flops 273275904 | bytes 21383824 | solution.py:105
  77.4 2.5 fusion.68
  82.9 2.0 collective-permute-start.1
  85.1 6.5 %collective-permute-done.2 = f32[4,64]{1,0:T(4,128)S(1)} collective-permute-done((f32[4,64]{1,0:T(4,128)S(1)}, f32[4,64]{1,0:T(4,128)S(1)}, u32[]{:S(2)}, u32[]{:S(2)}) %collective-permute-start.2) | collective-permute-done | bytes 1056 | tf_op jit(solution)/shard_map/while/body/eval_jaxpr/ppermute | solution.py:14
  93.3 2.5 fusion.68
  99.5 3.5 %collective-permute-start.3 = (f32[4,64]{1,0:T(4,128)S(1)}, f32[4,64]{1,0:T(4,128)S(1)}, u32[]{:S(2)}, u32[]{:S(2)}) collective-permute-start(f32[4,64]{1,0:T(4,128)S(1)} %get-tuple-element.509), channel_id=1, source_target_pairs={{0,1},{1,2},{2,3},{3,4},{4,5},{5,6},{6,7},{7,8},{8,9},{9,10},{10,1... | collective-permute-start | bytes 3080 | tf_op jit(solution)/shard_map/while/body/eval_jaxpr/ppermute | solution.py:14
  103.0 3.8 %collective-permute-done.2 = f32[4,64]{1,0:T(4,128)S(1)} collective-permute-done((f32[4,64]{1,0:T(4,128)S(1)}, f32[4,64]{1,0:T(4,128)S(1)}, u32[]{:S(2)}, u32[]{:S(2)}) %collective-permute-start.2) | collective-permute-done | bytes 1056 | tf_op jit(solution)/shard_map/while/body/eval_jaxpr/ppermute | solution.py:14
  108.4 2.5 fusion.68
  114.8 1.9 collective-permute-start.2
  118.0 3.8 %collective-permute-done.2 = f32[4,64]{1,0:T(4,128)S(1)} collective-permute-done((f32[4,64]{1,0:T(4,128)S(1)}, f32[4,64]{1,0:T(4,128)S(1)}, u32[]{:S(2)}, u32[]{:S(2)}) %collective-permute-start.2) | collective-permute-done | bytes 1056 | tf_op jit(solution)/shard_map/while/body/eval_jaxpr/ppermute | solution.py:14
  124.0 2.5 fusion.68
  130.8 1.9 collective-permute-start.3
  132.8 4.6 %collective-permute-done.2 = f32[4,64]{1,0:T(4,128)S(1)} collective-permute-done((f32[4,64]{1,0:T(4,128)S(1)}, f32[4,64]{1,0:T(4,128)S(1)}, u32[]{:S(2)}, u32[]{:S(2)}) %collective-permute-start.2) | collective-permute-done | bytes 1056 | tf_op jit(solution)/shard_map/while/body/eval_jaxpr/ppermute | solution.py:14
  139.0 2.5 fusion.68
  147.8 4.6 %collective-permute-done.2 = f32[4,64]{1,0:T(4,128)S(1)} collective-permute-done((f32[4,64]{1,0:T(4,128)S(1)}, f32[4,64]{1,0:T(4,128)S(1)}, u32[]{:S(2)}, u32[]{:S(2)}) %collective-permute-start.2) | collective-permute-done | bytes 1056 | tf_op jit(solution)/shard_map/while/body/eval_jaxpr/ppermute | solution.py:14
  154.1 2.5 fusion.68
  162.9 4.6 %collective-permute-done.2 = f32[4,64]{1,0:T(4,128)S(1)} collective-permute-done((f32[4,64]{1,0:T(4,128)S(1)}, f32[4,64]{1,0:T(4,128)S(1)}, u32[]{:S(2)}, u32[]{:S(2)}) %collective-permute-start.2) | collective-permute-done | bytes 1056 | tf_op jit(solution)/shard_map/while/body/eval_jaxpr/ppermute | solution.py:14
  169.1 2.5 fusion.68
  177.9 4.6 %collective-permute-done.2 = f32[4,64]{1,0:T(4,128)S(1)} collective-permute-done((f32[4,64]{1,0:T(4,128)S(1)}, f32[4,64]{1,0:T(4,128)S(1)}, u32[]{:S(2)}, u32[]{:S(2)}) %collective-permute-start.2) | collective-permute-done | bytes 1056 | tf_op jit(solution)/shard_map/while/body/eval_jaxpr/ppermute | solution.py:14
  184.2 2.5 fusion.68
  191.1 2.4 collective-permute-start.3
  193.5 4.1 %collective-permute-done.2 = f32[4,64]{1,0:T(4,128)S(1)} collective-permute-done((f32[4,64]{1,0:T(4,128)S(1)}, f32[4,64]{1,0:T(4,128)S(1)}, u32[]{:S(2)}, u32[]{:S(2)}) %collective-permute-start.2) | collective-permute-done | bytes 1056 | tf_op jit(solution)/shard_map/while/body/eval_jaxpr/ppermute | solution.py:14
  199.2 2.5 fusion.68
  206.1 2.4 collective-permute-start.3
  208.5 4.1 %collective-permute-done.2 = f32[4,64]{1,0:T(4,128)S(1)} collective-permute-done((f32[4,64]{1,0:T(4,128)S(1)}, f32[4,64]{1,0:T(4,128)S(1)}, u32[]{:S(2)}, u32[]{:S(2)}) %collective-permute-start.2) | collective-permute-done | bytes 1056 | tf_op jit(solution)/shard_map/while/body/eval_jaxpr/ppermute | solution.py:14
  214.2 2.5 fusion.68
  221.2 2.5 collective-permute-start.3
  223.6 4.0 %collective-permute-done.2 = f32[4,64]{1,0:T(4,128)S(1)} collective-permute-done((f32[4,64]{1,0:T(4,128)S(1)}, f32[4,64]{1,0:T(4,128)S(1)}, u32[]{:S(2)}, u32[]{:S(2)}) %collective-permute-start.2) | collective-permute-done | bytes 1056 | tf_op jit(solution)/shard_map/while/body/eval_jaxpr/ppermute | solution.py:14
  229.3 2.5 fusion.68
  236.2 2.5 collective-permute-start.3
  238.8 4.9 %collective-permute-done.2 = f32[4,64]{1,0:T(4,128)S(1)} collective-permute-done((f32[4,64]{1,0:T(4,128)S(1)}, f32[4,64]{1,0:T(4,128)S(1)}, u32[]{:S(2)}, u32[]{:S(2)}) %collective-permute-start.2) | collective-permute-done | bytes 1056 | tf_op jit(solution)/shard_map/while/body/eval_jaxpr/ppermute | solution.py:14
  245.3 2.5 fusion.68
  251.3 3.3 %collective-permute-start.3 = (f32[4,64]{1,0:T(4,128)S(1)}, f32[4,64]{1,0:T(4,128)S(1)}, u32[]{:S(2)}, u32[]{:S(2)}) collective-permute-start(f32[4,64]{1,0:T(4,128)S(1)} %get-tuple-element.509), channel_id=1, source_target_pairs={{0,1},{1,2},{2,3},{3,4},{4,5},{5,6},{6,7},{7,8},{8,9},{9,10},{10,1... | collective-permute-start | bytes 3080 | tf_op jit(solution)/shard_map/while/body/eval_jaxpr/ppermute | solution.py:14
  254.6 6.2 %collective-permute-done.2 = f32[4,64]{1,0:T(4,128)S(1)} collective-permute-done((f32[4,64]{1,0:T(4,128)S(1)}, f32[4,64]{1,0:T(4,128)S(1)}, u32[]{:S(2)}, u32[]{:S(2)}) %collective-permute-start.2) | collective-permute-done | bytes 1056 | tf_op jit(solution)/shard_map/while/body/eval_jaxpr/ppermute | solution.py:14
  262.4 2.5 fusion.68
  268.2 2.0 collective-permute-start.3
  270.2 7.0 %collective-permute-done.2 = f32[4,64]{1,0:T(4,128)S(1)} collective-permute-done((f32[4,64]{1,0:T(4,128)S(1)}, f32[4,64]{1,0:T(4,128)S(1)}, u32[]{:S(2)}, u32[]{:S(2)}) %collective-permute-start.2) | collective-permute-done | bytes 1056 | tf_op jit(solution)/shard_map/while/body/eval_jaxpr/ppermute | solution.py:14
  278.8 2.5 fusion.68
  285.2 7.5 %collective-permute-done.2 = f32[4,64]{1,0:T(4,128)S(1)} collective-permute-done((f32[4,64]{1,0:T(4,128)S(1)}, f32[4,64]{1,0:T(4,128)S(1)}, u32[]{:S(2)}, u32[]{:S(2)}) %collective-permute-start.2) | collective-permute-done | bytes 1056 | tf_op jit(solution)/shard_map/while/body/eval_jaxpr/ppermute | solution.py:14
  294.3 2.5 fusion.68
  301.8 5.9 %collective-permute-done.2 = f32[4,64]{1,0:T(4,128)S(1)} collective-permute-done((f32[4,64]{1,0:T(4,128)S(1)}, f32[4,64]{1,0:T(4,128)S(1)}, u32[]{:S(2)}, u32[]{:S(2)}) %collective-permute-start.2) | collective-permute-done | bytes 1056 | tf_op jit(solution)/shard_map/while/body/eval_jaxpr/ppermute | solution.py:14
  309.3 2.5 fusion.68
  315.1 2.4 collective-permute-start.3
  317.6 5.2 %collective-permute-done.2 = f32[4,64]{1,0:T(4,128)S(1)} collective-permute-done((f32[4,64]{1,0:T(4,128)S(1)}, f32[4,64]{1,0:T(4,128)S(1)}, u32[]{:S(2)}, u32[]{:S(2)}) %collective-permute-start.2) | collective-permute-done | bytes 1056 | tf_op jit(solution)/shard_map/while/body/eval_jaxpr/ppermute | solution.py:14
  (417 shorter events, 90.1 us)
Async XLA Ops:
  82.9 8.8 %collective-permute-start.1 = (f32[4,8192]{1,0:T(4,128)S(1)}, f32[4,8192]{1,0:T(4,128)S(1)}, u32[]{:S(2)}, u32[]{:S(2)}) collective-permute-start(f32[4,8192]{1,0:T(4,128)S(1)} %fusion.71), channel_id=1, source_target_pairs={{0,1},{1,2},{2,3},{3,4},{4,5},{5,6},{6,7},{7,8},{8,9},{9,10},{10,1... | collective-permute-start | bytes 393224 | tf_op jit(solution)/shard_map/while/body/eval_jaxpr/ppermute | solution.py:14
  84.9 6.8 %collective-permute-start = (bf16[4,8192]{1,0:T(4,128)(2,1)S(1)}, bf16[4,8192]{1,0:T(4,128)(2,1)S(1)}, u32[]{:S(2)}, u32[]{:S(2)}) collective-permute-start(bf16[4,8192]{1,0:T(4,128)(2,1)S(1)} %copy.160), channel_id=1, source_target_pairs={{0,1},{1,2},{2,3},{3,4},{4,5},{5,6},{6,7},{7,8},{8,9},{9,10},{10,1... | collective-permute-start | bytes 196616 | tf_op jit(solution)/shard_map/while/body/eval_jaxpr/ppermute | solution.py:14
  85.0 6.7 %collective-permute-start.2 = (f32[4,64]{1,0:T(4,128)S(1)}, f32[4,64]{1,0:T(4,128)S(1)}, u32[]{:S(2)}, u32[]{:S(2)}) collective-permute-start(f32[4,64]{1,0:T(4,128)S(1)} %get-tuple-element.508), channel_id=1, source_target_pairs={{0,1},{1,2},{2,3},{3,4},{4,5},{5,6},{6,7},{7,8},{8,9},{9,10},{10,1... | collective-permute-start | bytes 3080 | tf_op jit(solution)/shard_map/while/body/eval_jaxpr/ppermute | solution.py:14
  98.9 8.0 %collective-permute-start.1 = (f32[4,8192]{1,0:T(4,128)S(1)}, f32[4,8192]{1,0:T(4,128)S(1)}, u32[]{:S(2)}, u32[]{:S(2)}) collective-permute-start(f32[4,8192]{1,0:T(4,128)S(1)} %fusion.71), channel_id=1, source_target_pairs={{0,1},{1,2},{2,3},{3,4},{4,5},{5,6},{6,7},{7,8},{8,9},{9,10},{10,1... | collective-permute-start | bytes 393224 | tf_op jit(solution)/shard_map/while/body/eval_jaxpr/ppermute | solution.py:14
  98.9 7.9 %collective-permute-start = (bf16[4,8192]{1,0:T(4,128)(2,1)S(1)}, bf16[4,8192]{1,0:T(4,128)(2,1)S(1)}, u32[]{:S(2)}, u32[]{:S(2)}) collective-permute-start(bf16[4,8192]{1,0:T(4,128)(2,1)S(1)} %copy.160), channel_id=1, source_target_pairs={{0,1},{1,2},{2,3},{3,4},{4,5},{5,6},{6,7},{7,8},{8,9},{9,10},{10,1... | collective-permute-start | bytes 196616 | tf_op jit(solution)/shard_map/while/body/eval_jaxpr/ppermute | solution.py:14
  99.0 7.7 %collective-permute-start.2 = (f32[4,64]{1,0:T(4,128)S(1)}, f32[4,64]{1,0:T(4,128)S(1)}, u32[]{:S(2)}, u32[]{:S(2)}) collective-permute-start(f32[4,64]{1,0:T(4,128)S(1)} %get-tuple-element.508), channel_id=1, source_target_pairs={{0,1},{1,2},{2,3},{3,4},{4,5},{5,6},{6,7},{7,8},{8,9},{9,10},{10,1... | collective-permute-start | bytes 3080 | tf_op jit(solution)/shard_map/while/body/eval_jaxpr/ppermute | solution.py:14
  99.5 7.3 %collective-permute-start.3 = (f32[4,64]{1,0:T(4,128)S(1)}, f32[4,64]{1,0:T(4,128)S(1)}, u32[]{:S(2)}, u32[]{:S(2)}) collective-permute-start(f32[4,64]{1,0:T(4,128)S(1)} %get-tuple-element.509), channel_id=1, source_target_pairs={{0,1},{1,2},{2,3},{3,4},{4,5},{5,6},{6,7},{7,8},{8,9},{9,10},{10,1... | collective-permute-start | bytes 3080 | tf_op jit(solution)/shard_map/while/body/eval_jaxpr/ppermute | solution.py:14
  113.9 8.5 %collective-permute-start.1 = (f32[4,8192]{1,0:T(4,128)S(1)}, f32[4,8192]{1,0:T(4,128)S(1)}, u32[]{:S(2)}, u32[]{:S(2)}) collective-permute-start(f32[4,8192]{1,0:T(4,128)S(1)} %fusion.71), channel_id=1, source_target_pairs={{0,1},{1,2},{2,3},{3,4},{4,5},{5,6},{6,7},{7,8},{8,9},{9,10},{10,1... | collective-permute-start | bytes 393224 | tf_op jit(solution)/shard_map/while/body/eval_jaxpr/ppermute | solution.py:14
  114.0 8.4 %collective-permute-start = (bf16[4,8192]{1,0:T(4,128)(2,1)S(1)}, bf16[4,8192]{1,0:T(4,128)(2,1)S(1)}, u32[]{:S(2)}, u32[]{:S(2)}) collective-permute-start(bf16[4,8192]{1,0:T(4,128)(2,1)S(1)} %copy.160), channel_id=1, source_target_pairs={{0,1},{1,2},{2,3},{3,4},{4,5},{5,6},{6,7},{7,8},{8,9},{9,10},{10,1... | collective-permute-start | bytes 196616 | tf_op jit(solution)/shard_map/while/body/eval_jaxpr/ppermute | solution.py:14
  114.8 7.0 %collective-permute-start.2 = (f32[4,64]{1,0:T(4,128)S(1)}, f32[4,64]{1,0:T(4,128)S(1)}, u32[]{:S(2)}, u32[]{:S(2)}) collective-permute-start(f32[4,64]{1,0:T(4,128)S(1)} %get-tuple-element.508), channel_id=1, source_target_pairs={{0,1},{1,2},{2,3},{3,4},{4,5},{5,6},{6,7},{7,8},{8,9},{9,10},{10,1... | collective-permute-start | bytes 3080 | tf_op jit(solution)/shard_map/while/body/eval_jaxpr/ppermute | solution.py:14
  129.5 7.9 %collective-permute-start.1 = (f32[4,8192]{1,0:T(4,128)S(1)}, f32[4,8192]{1,0:T(4,128)S(1)}, u32[]{:S(2)}, u32[]{:S(2)}) collective-permute-start(f32[4,8192]{1,0:T(4,128)S(1)} %fusion.71), channel_id=1, source_target_pairs={{0,1},{1,2},{2,3},{3,4},{4,5},{5,6},{6,7},{7,8},{8,9},{9,10},{10,1... | collective-permute-start | bytes 393224 | tf_op jit(solution)/shard_map/while/body/eval_jaxpr/ppermute | solution.py:14
  129.6 7.8 %collective-permute-start = (bf16[4,8192]{1,0:T(4,128)(2,1)S(1)}, bf16[4,8192]{1,0:T(4,128)(2,1)S(1)}, u32[]{:S(2)}, u32[]{:S(2)}) collective-permute-start(bf16[4,8192]{1,0:T(4,128)(2,1)S(1)} %copy.160), channel_id=1, source_target_pairs={{0,1},{1,2},{2,3},{3,4},{4,5},{5,6},{6,7},{7,8},{8,9},{9,10},{10,1... | collective-permute-start | bytes 196616 | tf_op jit(solution)/shard_map/while/body/eval_jaxpr/ppermute | solution.py:14
  144.6 7.9 %collective-permute-start.1 = (f32[4,8192]{1,0:T(4,128)S(1)}, f32[4,8192]{1,0:T(4,128)S(1)}, u32[]{:S(2)}, u32[]{:S(2)}) collective-permute-start(f32[4,8192]{1,0:T(4,128)S(1)} %fusion.71), channel_id=1, source_target_pairs={{0,1},{1,2},{2,3},{3,4},{4,5},{5,6},{6,7},{7,8},{8,9},{9,10},{10,1... | collective-permute-start | bytes 393224 | tf_op jit(solution)/shard_map/while/body/eval_jaxpr/ppermute | solution.py:14
  144.7 7.8 %collective-permute-start = (bf16[4,8192]{1,0:T(4,128)(2,1)S(1)}, bf16[4,8192]{1,0:T(4,128)(2,1)S(1)}, u32[]{:S(2)}, u32[]{:S(2)}) collective-permute-start(bf16[4,8192]{1,0:T(4,128)(2,1)S(1)} %copy.160), channel_id=1, source_target_pairs={{0,1},{1,2},{2,3},{3,4},{4,5},{5,6},{6,7},{7,8},{8,9},{9,10},{10,1... | collective-permute-start | bytes 196616 | tf_op jit(solution)/shard_map/while/body/eval_jaxpr/ppermute | solution.py:14
  159.6 7.9 %collective-permute-start.1 = (f32[4,8192]{1,0:T(4,128)S(1)}, f32[4,8192]{1,0:T(4,128)S(1)}, u32[]{:S(2)}, u32[]{:S(2)}) collective-permute-start(f32[4,8192]{1,0:T(4,128)S(1)} %fusion.71), channel_id=1, source_target_pairs={{0,1},{1,2},{2,3},{3,4},{4,5},{5,6},{6,7},{7,8},{8,9},{9,10},{10,1... | collective-permute-start | bytes 393224 | tf_op jit(solution)/shard_map/while/body/eval_jaxpr/ppermute | solution.py:14
  159.7 7.8 %collective-permute-start = (bf16[4,8192]{1,0:T(4,128)(2,1)S(1)}, bf16[4,8192]{1,0:T(4,128)(2,1)S(1)}, u32[]{:S(2)}, u32[]{:S(2)}) collective-permute-start(bf16[4,8192]{1,0:T(4,128)(2,1)S(1)} %copy.160), channel_id=1, source_target_pairs={{0,1},{1,2},{2,3},{3,4},{4,5},{5,6},{6,7},{7,8},{8,9},{9,10},{10,1... | collective-permute-start | bytes 196616 | tf_op jit(solution)/shard_map/while/body/eval_jaxpr/ppermute | solution.py:14
  174.6 7.9 %collective-permute-start.1 = (f32[4,8192]{1,0:T(4,128)S(1)}, f32[4,8192]{1,0:T(4,128)S(1)}, u32[]{:S(2)}, u32[]{:S(2)}) collective-permute-start(f32[4,8192]{1,0:T(4,128)S(1)} %fusion.71), channel_id=1, source_target_pairs={{0,1},{1,2},{2,3},{3,4},{4,5},{5,6},{6,7},{7,8},{8,9},{9,10},{10,1... | collective-permute-start | bytes 393224 | tf_op jit(solution)/shard_map/while/body/eval_jaxpr/ppermute | solution.py:14
  174.7 7.8 %collective-permute-start = (bf16[4,8192]{1,0:T(4,128)(2,1)S(1)}, bf16[4,8192]{1,0:T(4,128)(2,1)S(1)}, u32[]{:S(2)}, u32[]{:S(2)}) collective-permute-start(bf16[4,8192]{1,0:T(4,128)(2,1)S(1)} %copy.160), channel_id=1, source_target_pairs={{0,1},{1,2},{2,3},{3,4},{4,5},{5,6},{6,7},{7,8},{8,9},{9,10},{10,1... | collective-permute-start | bytes 196616 | tf_op jit(solution)/shard_map/while/body/eval_jaxpr/ppermute | solution.py:14
  189.7 7.9 %collective-permute-start.1 = (f32[4,8192]{1,0:T(4,128)S(1)}, f32[4,8192]{1,0:T(4,128)S(1)}, u32[]{:S(2)}, u32[]{:S(2)}) collective-permute-start(f32[4,8192]{1,0:T(4,128)S(1)} %fusion.71), channel_id=1, source_target_pairs={{0,1},{1,2},{2,3},{3,4},{4,5},{5,6},{6,7},{7,8},{8,9},{9,10},{10,1... | collective-permute-start | bytes 393224 | tf_op jit(solution)/shard_map/while/body/eval_jaxpr/ppermute | solution.py:14
  189.8 7.8 %collective-permute-start = (bf16[4,8192]{1,0:T(4,128)(2,1)S(1)}, bf16[4,8192]{1,0:T(4,128)(2,1)S(1)}, u32[]{:S(2)}, u32[]{:S(2)}) collective-permute-start(bf16[4,8192]{1,0:T(4,128)(2,1)S(1)} %copy.160), channel_id=1, source_target_pairs={{0,1},{1,2},{2,3},{3,4},{4,5},{5,6},{6,7},{7,8},{8,9},{9,10},{10,1... | collective-permute-start | bytes 196616 | tf_op jit(solution)/shard_map/while/body/eval_jaxpr/ppermute | solution.py:14
  204.7 7.9 %collective-permute-start.1 = (f32[4,8192]{1,0:T(4,128)S(1)}, f32[4,8192]{1,0:T(4,128)S(1)}, u32[]{:S(2)}, u32[]{:S(2)}) collective-permute-start(f32[4,8192]{1,0:T(4,128)S(1)} %fusion.71), channel_id=1, source_target_pairs={{0,1},{1,2},{2,3},{3,4},{4,5},{5,6},{6,7},{7,8},{8,9},{9,10},{10,1... | collective-permute-start | bytes 393224 | tf_op jit(solution)/shard_map/while/body/eval_jaxpr/ppermute | solution.py:14
  204.8 7.8 %collective-permute-start = (bf16[4,8192]{1,0:T(4,128)(2,1)S(1)}, bf16[4,8192]{1,0:T(4,128)(2,1)S(1)}, u32[]{:S(2)}, u32[]{:S(2)}) collective-permute-start(bf16[4,8192]{1,0:T(4,128)(2,1)S(1)} %copy.160), channel_id=1, source_target_pairs={{0,1},{1,2},{2,3},{3,4},{4,5},{5,6},{6,7},{7,8},{8,9},{9,10},{10,1... | collective-permute-start | bytes 196616 | tf_op jit(solution)/shard_map/while/body/eval_jaxpr/ppermute | solution.py:14
  219.8 7.9 %collective-permute-start.1 = (f32[4,8192]{1,0:T(4,128)S(1)}, f32[4,8192]{1,0:T(4,128)S(1)}, u32[]{:S(2)}, u32[]{:S(2)}) collective-permute-start(f32[4,8192]{1,0:T(4,128)S(1)} %fusion.71), channel_id=1, source_target_pairs={{0,1},{1,2},{2,3},{3,4},{4,5},{5,6},{6,7},{7,8},{8,9},{9,10},{10,1... | collective-permute-start | bytes 393224 | tf_op jit(solution)/shard_map/while/body/eval_jaxpr/ppermute | solution.py:14
  219.9 7.8 %collective-permute-start = (bf16[4,8192]{1,0:T(4,128)(2,1)S(1)}, bf16[4,8192]{1,0:T(4,128)(2,1)S(1)}, u32[]{:S(2)}, u32[]{:S(2)}) collective-permute-start(bf16[4,8192]{1,0:T(4,128)(2,1)S(1)} %copy.160), channel_id=1, source_target_pairs={{0,1},{1,2},{2,3},{3,4},{4,5},{5,6},{6,7},{7,8},{8,9},{9,10},{10,1... | collective-permute-start | bytes 196616 | tf_op jit(solution)/shard_map/while/body/eval_jaxpr/ppermute | solution.py:14
  234.8 8.9 %collective-permute-start.1 = (f32[4,8192]{1,0:T(4,128)S(1)}, f32[4,8192]{1,0:T(4,128)S(1)}, u32[]{:S(2)}, u32[]{:S(2)}) collective-permute-start(f32[4,8192]{1,0:T(4,128)S(1)} %fusion.71), channel_id=1, source_target_pairs={{0,1},{1,2},{2,3},{3,4},{4,5},{5,6},{6,7},{7,8},{8,9},{9,10},{10,1... | collective-permute-start | bytes 393224 | tf_op jit(solution)/shard_map/while/body/eval_jaxpr/ppermute | solution.py:14
  234.9 8.8 %collective-permute-start = (bf16[4,8192]{1,0:T(4,128)(2,1)S(1)}, bf16[4,8192]{1,0:T(4,128)(2,1)S(1)}, u32[]{:S(2)}, u32[]{:S(2)}) collective-permute-start(bf16[4,8192]{1,0:T(4,128)(2,1)S(1)} %copy.160), channel_id=1, source_target_pairs={{0,1},{1,2},{2,3},{3,4},{4,5},{5,6},{6,7},{7,8},{8,9},{9,10},{10,1... | collective-permute-start | bytes 196616 | tf_op jit(solution)/shard_map/while/body/eval_jaxpr/ppermute | solution.py:14
  236.1 7.5 %collective-permute-start.2 = (f32[4,64]{1,0:T(4,128)S(1)}, f32[4,64]{1,0:T(4,128)S(1)}, u32[]{:S(2)}, u32[]{:S(2)}) collective-permute-start(f32[4,64]{1,0:T(4,128)S(1)} %get-tuple-element.508), channel_id=1, source_target_pairs={{0,1},{1,2},{2,3},{3,4},{4,5},{5,6},{6,7},{7,8},{8,9},{9,10},{10,1... | collective-permute-start | bytes 3080 | tf_op jit(solution)/shard_map/while/body/eval_jaxpr/ppermute | solution.py:14
  236.2 7.5 %collective-permute-start.3 = (f32[4,64]{1,0:T(4,128)S(1)}, f32[4,64]{1,0:T(4,128)S(1)}, u32[]{:S(2)}, u32[]{:S(2)}) collective-permute-start(f32[4,64]{1,0:T(4,128)S(1)} %get-tuple-element.509), channel_id=1, source_target_pairs={{0,1},{1,2},{2,3},{3,4},{4,5},{5,6},{6,7},{7,8},{8,9},{9,10},{10,1... | collective-permute-start | bytes 3080 | tf_op jit(solution)/shard_map/while/body/eval_jaxpr/ppermute | solution.py:14
  250.8 10.0 %collective-permute-start.1 = (f32[4,8192]{1,0:T(4,128)S(1)}, f32[4,8192]{1,0:T(4,128)S(1)}, u32[]{:S(2)}, u32[]{:S(2)}) collective-permute-start(f32[4,8192]{1,0:T(4,128)S(1)} %fusion.71), channel_id=1, source_target_pairs={{0,1},{1,2},{2,3},{3,4},{4,5},{5,6},{6,7},{7,8},{8,9},{9,10},{10,1... | collective-permute-start | bytes 393224 | tf_op jit(solution)/shard_map/while/body/eval_jaxpr/ppermute | solution.py:14
  250.9 9.9 %collective-permute-start = (bf16[4,8192]{1,0:T(4,128)(2,1)S(1)}, bf16[4,8192]{1,0:T(4,128)(2,1)S(1)}, u32[]{:S(2)}, u32[]{:S(2)}) collective-permute-start(bf16[4,8192]{1,0:T(4,128)(2,1)S(1)} %copy.160), channel_id=1, source_target_pairs={{0,1},{1,2},{2,3},{3,4},{4,5},{5,6},{6,7},{7,8},{8,9},{9,10},{10,1... | collective-permute-start | bytes 196616 | tf_op jit(solution)/shard_map/while/body/eval_jaxpr/ppermute | solution.py:14
  251.2 9.6 %collective-permute-start.2 = (f32[4,64]{1,0:T(4,128)S(1)}, f32[4,64]{1,0:T(4,128)S(1)}, u32[]{:S(2)}, u32[]{:S(2)}) collective-permute-start(f32[4,64]{1,0:T(4,128)S(1)} %get-tuple-element.508), channel_id=1, source_target_pairs={{0,1},{1,2},{2,3},{3,4},{4,5},{5,6},{6,7},{7,8},{8,9},{9,10},{10,1... | collective-permute-start | bytes 3080 | tf_op jit(solution)/shard_map/while/body/eval_jaxpr/ppermute | solution.py:14
  251.3 9.6 %collective-permute-start.3 = (f32[4,64]{1,0:T(4,128)S(1)}, f32[4,64]{1,0:T(4,128)S(1)}, u32[]{:S(2)}, u32[]{:S(2)}) collective-permute-start(f32[4,64]{1,0:T(4,128)S(1)} %get-tuple-element.509), channel_id=1, source_target_pairs={{0,1},{1,2},{2,3},{3,4},{4,5},{5,6},{6,7},{7,8},{8,9},{9,10},{10,1... | collective-permute-start | bytes 3080 | tf_op jit(solution)/shard_map/while/body/eval_jaxpr/ppermute | solution.py:14
  268.0 9.2 %collective-permute-start.1 = (f32[4,8192]{1,0:T(4,128)S(1)}, f32[4,8192]{1,0:T(4,128)S(1)}, u32[]{:S(2)}, u32[]{:S(2)}) collective-permute-start(f32[4,8192]{1,0:T(4,128)S(1)} %fusion.71), channel_id=1, source_target_pairs={{0,1},{1,2},{2,3},{3,4},{4,5},{5,6},{6,7},{7,8},{8,9},{9,10},{10,1... | collective-permute-start | bytes 393224 | tf_op jit(solution)/shard_map/while/body/eval_jaxpr/ppermute | solution.py:14
  268.1 9.1 %collective-permute-start = (bf16[4,8192]{1,0:T(4,128)(2,1)S(1)}, bf16[4,8192]{1,0:T(4,128)(2,1)S(1)}, u32[]{:S(2)}, u32[]{:S(2)}) collective-permute-start(bf16[4,8192]{1,0:T(4,128)(2,1)S(1)} %copy.160), channel_id=1, source_target_pairs={{0,1},{1,2},{2,3},{3,4},{4,5},{5,6},{6,7},{7,8},{8,9},{9,10},{10,1... | collective-permute-start | bytes 196616 | tf_op jit(solution)/shard_map/while/body/eval_jaxpr/ppermute | solution.py:14
  268.1 9.0 %collective-permute-start.2 = (f32[4,64]{1,0:T(4,128)S(1)}, f32[4,64]{1,0:T(4,128)S(1)}, u32[]{:S(2)}, u32[]{:S(2)}) collective-permute-start(f32[4,64]{1,0:T(4,128)S(1)} %get-tuple-element.508), channel_id=1, source_target_pairs={{0,1},{1,2},{2,3},{3,4},{4,5},{5,6},{6,7},{7,8},{8,9},{9,10},{10,1... | collective-permute-start | bytes 3080 | tf_op jit(solution)/shard_map/while/body/eval_jaxpr/ppermute | solution.py:14
  268.2 9.0 %collective-permute-start.3 = (f32[4,64]{1,0:T(4,128)S(1)}, f32[4,64]{1,0:T(4,128)S(1)}, u32[]{:S(2)}, u32[]{:S(2)}) collective-permute-start(f32[4,64]{1,0:T(4,128)S(1)} %get-tuple-element.509), channel_id=1, source_target_pairs={{0,1},{1,2},{2,3},{3,4},{4,5},{5,6},{6,7},{7,8},{8,9},{9,10},{10,1... | collective-permute-start | bytes 3080 | tf_op jit(solution)/shard_map/while/body/eval_jaxpr/ppermute | solution.py:14
  284.3 8.4 %collective-permute-start.1 = (f32[4,8192]{1,0:T(4,128)S(1)}, f32[4,8192]{1,0:T(4,128)S(1)}, u32[]{:S(2)}, u32[]{:S(2)}) collective-permute-start(f32[4,8192]{1,0:T(4,128)S(1)} %fusion.71), channel_id=1, source_target_pairs={{0,1},{1,2},{2,3},{3,4},{4,5},{5,6},{6,7},{7,8},{8,9},{9,10},{10,1... | collective-permute-start | bytes 393224 | tf_op jit(solution)/shard_map/while/body/eval_jaxpr/ppermute | solution.py:14
  284.4 8.3 %collective-permute-start = (bf16[4,8192]{1,0:T(4,128)(2,1)S(1)}, bf16[4,8192]{1,0:T(4,128)(2,1)S(1)}, u32[]{:S(2)}, u32[]{:S(2)}) collective-permute-start(bf16[4,8192]{1,0:T(4,128)(2,1)S(1)} %copy.160), channel_id=1, source_target_pairs={{0,1},{1,2},{2,3},{3,4},{4,5},{5,6},{6,7},{7,8},{8,9},{9,10},{10,1... | collective-permute-start | bytes 196616 | tf_op jit(solution)/shard_map/while/body/eval_jaxpr/ppermute | solution.py:14
  284.5 8.2 %collective-permute-start.2 = (f32[4,64]{1,0:T(4,128)S(1)}, f32[4,64]{1,0:T(4,128)S(1)}, u32[]{:S(2)}, u32[]{:S(2)}) collective-permute-start(f32[4,64]{1,0:T(4,128)S(1)} %get-tuple-element.508), channel_id=1, source_target_pairs={{0,1},{1,2},{2,3},{3,4},{4,5},{5,6},{6,7},{7,8},{8,9},{9,10},{10,1... | collective-permute-start | bytes 3080 | tf_op jit(solution)/shard_map/while/body/eval_jaxpr/ppermute | solution.py:14
  284.6 8.1 %collective-permute-start.3 = (f32[4,64]{1,0:T(4,128)S(1)}, f32[4,64]{1,0:T(4,128)S(1)}, u32[]{:S(2)}, u32[]{:S(2)}) collective-permute-start(f32[4,64]{1,0:T(4,128)S(1)} %get-tuple-element.509), channel_id=1, source_target_pairs={{0,1},{1,2},{2,3},{3,4},{4,5},{5,6},{6,7},{7,8},{8,9},{9,10},{10,1... | collective-permute-start | bytes 3080 | tf_op jit(solution)/shard_map/while/body/eval_jaxpr/ppermute | solution.py:14
  299.8 7.9 %collective-permute-start.1 = (f32[4,8192]{1,0:T(4,128)S(1)}, f32[4,8192]{1,0:T(4,128)S(1)}, u32[]{:S(2)}, u32[]{:S(2)}) collective-permute-start(f32[4,8192]{1,0:T(4,128)S(1)} %fusion.71), channel_id=1, source_target_pairs={{0,1},{1,2},{2,3},{3,4},{4,5},{5,6},{6,7},{7,8},{8,9},{9,10},{10,1... | collective-permute-start | bytes 393224 | tf_op jit(solution)/shard_map/while/body/eval_jaxpr/ppermute | solution.py:14
  299.9 7.8 %collective-permute-start = (bf16[4,8192]{1,0:T(4,128)(2,1)S(1)}, bf16[4,8192]{1,0:T(4,128)(2,1)S(1)}, u32[]{:S(2)}, u32[]{:S(2)}) collective-permute-start(bf16[4,8192]{1,0:T(4,128)(2,1)S(1)} %copy.160), channel_id=1, source_target_pairs={{0,1},{1,2},{2,3},{3,4},{4,5},{5,6},{6,7},{7,8},{8,9},{9,10},{10,1... | collective-permute-start | bytes 196616 | tf_op jit(solution)/shard_map/while/body/eval_jaxpr/ppermute | solution.py:14
  300.0 7.7 %collective-permute-start.2 = (f32[4,64]{1,0:T(4,128)S(1)}, f32[4,64]{1,0:T(4,128)S(1)}, u32[]{:S(2)}, u32[]{:S(2)}) collective-permute-start(f32[4,64]{1,0:T(4,128)S(1)} %get-tuple-element.508), channel_id=1, source_target_pairs={{0,1},{1,2},{2,3},{3,4},{4,5},{5,6},{6,7},{7,8},{8,9},{9,10},{10,1... | collective-permute-start | bytes 3080 | tf_op jit(solution)/shard_map/while/body/eval_jaxpr/ppermute | solution.py:14
  300.1 7.6 %collective-permute-start.3 = (f32[4,64]{1,0:T(4,128)S(1)}, f32[4,64]{1,0:T(4,128)S(1)}, u32[]{:S(2)}, u32[]{:S(2)}) collective-permute-start(f32[4,64]{1,0:T(4,128)S(1)} %get-tuple-element.509), channel_id=1, source_target_pairs={{0,1},{1,2},{2,3},{3,4},{4,5},{5,6},{6,7},{7,8},{8,9},{9,10},{10,1... | collective-permute-start | bytes 3080 | tf_op jit(solution)/shard_map/while/body/eval_jaxpr/ppermute | solution.py:14
  314.9 7.9 %collective-permute-start.1 = (f32[4,8192]{1,0:T(4,128)S(1)}, f32[4,8192]{1,0:T(4,128)S(1)}, u32[]{:S(2)}, u32[]{:S(2)}) collective-permute-start(f32[4,8192]{1,0:T(4,128)S(1)} %fusion.71), channel_id=1, source_target_pairs={{0,1},{1,2},{2,3},{3,4},{4,5},{5,6},{6,7},{7,8},{8,9},{9,10},{10,1... | collective-permute-start | bytes 393224 | tf_op jit(solution)/shard_map/while/body/eval_jaxpr/ppermute | solution.py:14
  315.0 7.8 %collective-permute-start = (bf16[4,8192]{1,0:T(4,128)(2,1)S(1)}, bf16[4,8192]{1,0:T(4,128)(2,1)S(1)}, u32[]{:S(2)}, u32[]{:S(2)}) collective-permute-start(bf16[4,8192]{1,0:T(4,128)(2,1)S(1)} %copy.160), channel_id=1, source_target_pairs={{0,1},{1,2},{2,3},{3,4},{4,5},{5,6},{6,7},{7,8},{8,9},{9,10},{10,1... | collective-permute-start | bytes 196616 | tf_op jit(solution)/shard_map/while/body/eval_jaxpr/ppermute | solution.py:14
  315.0 7.7 %collective-permute-start.2 = (f32[4,64]{1,0:T(4,128)S(1)}, f32[4,64]{1,0:T(4,128)S(1)}, u32[]{:S(2)}, u32[]{:S(2)}) collective-permute-start(f32[4,64]{1,0:T(4,128)S(1)} %get-tuple-element.508), channel_id=1, source_target_pairs={{0,1},{1,2},{2,3},{3,4},{4,5},{5,6},{6,7},{7,8},{8,9},{9,10},{10,1... | collective-permute-start | bytes 3080 | tf_op jit(solution)/shard_map/while/body/eval_jaxpr/ppermute | solution.py:14
  315.1 7.6 %collective-permute-start.3 = (f32[4,64]{1,0:T(4,128)S(1)}, f32[4,64]{1,0:T(4,128)S(1)}, u32[]{:S(2)}, u32[]{:S(2)}) collective-permute-start(f32[4,64]{1,0:T(4,128)S(1)} %get-tuple-element.509), channel_id=1, source_target_pairs={{0,1},{1,2},{2,3},{3,4},{4,5},{5,6},{6,7},{7,8},{8,9},{9,10},{10,1... | collective-permute-start | bytes 3080 | tf_op jit(solution)/shard_map/while/body/eval_jaxpr/ppermute | solution.py:14
  (33 other events, 133.9 us)
where the time goes:
time: 326 us; the launch traced here: 324 us
  waiting for transfers between devices  82.5 us (25%)
  blocking collectives  66.1 us (20%)
  matrix products  53.6 us (16%)
  starting transfers between devices  50.2 us (15%)
  local copies, waits for them, and re-layouts  29.6 us (9%)
  other arithmetic  29.3 us (9%)
  loops' own time  12.3 us (4%)
    ppermute x64, waiting for transfers between devices, from_behind(): lax.ppermute(x, axis, [(i, (i + by) % devices) for i in range(devices)])  82.5 us
    ppermute x64, starting transfers between devices, from_behind(): lax.ppermute(x, axis, [(i, (i + by) % devices) for i in range(devices)])  50.2 us
    dot_general x17, matrix products, attend(): jnp.einsum('rkgd,nkd->rkgn', grouped, keys_grouped, preferred_element_typ...  40.8 us
    all_gather x1, blocking collectives, local(): keys_piece = lax.all_gather(new_keys, 'ctx', axis=0, tiled=True)  35.9 us
    all_gather x1, blocking collectives, local(): values_piece = lax.all_gather(new_values, 'ctx', axis=0, tiled=True)  30.2 us
    while x80, local copies, waits for them, and re-layouts  19 us
    dot_general x17, matrix products, attend(): jnp.einsum('rkgn,nkd->rkgd', weights.astype(jnp.bfloat16), values_grouped...  12.8 us
    another operation x1, loops' own time, local(): lax.fori_loop(0, count, hop_one, (queries,) + empty_state(rows, heads))  12.3 us
  transfers between devices with their start and end apart: 64, of which 17 were waited for; matrix products, arithmetic and copies ran while one was open for 0% of the time, Pallas kernels for 0%

commit v1 on v0

--- a/solution.py
+++ b/solution.py
@@ -87,7 +87,10 @@
         return attend(held, positions, cache_keys, cache_values, cache_pos, cache_live)
 
     keys_piece = lax.all_gather(new_keys, "ctx", axis=0, tiled=True)
-    values_piece = lax.all_gather(new_values, "ctx", axis=0, tiled=True)
+    size = lax.axis_size("ctx")
+    pieces = jnp.stack([new_values for _ in range(size)])
+    pieces = lax.all_to_all(pieces, "ctx", split_axis=0, concat_axis=0)
+    values_piece = jnp.concatenate(pieces, axis=0)
     piece_rows = keys_piece.shape[0]
     key_pos = length + lax.iota(jnp.int32, piece_rows)
     span_state = combine(

time: 326 us -> 303 us (0.929)
  blocking collectives: 66.1 us -> 32.8 us
  starting transfers between devices: 50.2 us -> 67.1 us
  waiting for transfers between devices: 82.5 us -> 73.5 us
    all_gather x1 -> x0, blocking collectives: 30.2 us -> none  [local(): values_piece = lax.all_gather(new_values, 'ctx', axis=0, tiled=True)]
    all_to_all x0 -> x1, starting transfers between devices: none -> 9.94 us  [local(): pieces = lax.all_to_all(pieces, 'ctx', split_axis=0, concat_axis=0)]
    ppermute x64, waiting for transfers between devices: 82.5 us -> 73.5 us  [from_behind(): lax.ppermute(x, axis, [(i, (i + by) % devices) for i in range(devices)])]
    ppermute x64, starting transfers between devices: 50.2 us -> 57.1 us  [from_behind(): lax.ppermute(x, axis, [(i, (i + by) % devices) for i in range(devices)])]
  transfers between devices with their start and end apart: 64 -> 65, of which waited for: 17 -> 16; matrix products, arithmetic and copies ran while one was open for 0% -> 31% of each run, Pallas kernels for 0% -> 0%
where the time goes in v1:
time: 303 us; the launch traced here: 300 us
  waiting for transfers between devices  73.5 us (24%)
  starting transfers between devices  67.1 us (22%)
  matrix products  53.6 us (18%)
  blocking collectives  32.8 us (11%)
  local copies, waits for them, and re-layouts  30.9 us (10%)
  other arithmetic  29.3 us (10%)
  loops' own time  12.3 us (4%)
    ppermute x64, waiting for transfers between devices, from_behind(): lax.ppermute(x, axis, [(i, (i + by) % devices) for i in range(devices)])  73.5 us
    ppermute x64, starting transfers between devices, from_behind(): lax.ppermute(x, axis, [(i, (i + by) % devices) for i in range(devices)])  57.1 us
    dot_general x17, matrix products, attend(): jnp.einsum('rkgd,nkd->rkgn', grouped, keys_grouped, preferred_element_typ...  40.8 us
    all_gather x1, blocking collectives, local(): keys_piece = lax.all_gather(new_keys, 'ctx', axis=0, tiled=True)  32.8 us
    while x80, local copies, waits for them, and re-layouts  19 us
    dot_general x17, matrix products, attend(): jnp.einsum('rkgn,nkd->rkgd', weights.astype(jnp.bfloat16), values_grouped...  12.8 us
    another operation x1, loops' own time, local(): lax.fori_loop(0, count, hop_one, (queries,) + empty_state(rows, heads))  12.3 us
    lt x16, other arithmetic, local(): cache_live = cache_pos < length  11.5 us
  transfers between devices with their start and end apart: 65, of which 16 were waited for; matrix products, arithmetic and copies ran while one was open for 31% of the time, Pallas kernels for 0%

profile of v1, /device:TPU:2, one launch (start us, length us, event | category | flops | bytes accessed | tf_op | source)
XLA Modules:
  0.0 300.1 jit_solution(971745505742986761)
XLA Ops:
  2.2 9.9 %all-to-all-start = ((bf16[16,4,512]{2,1,0:T(4,128)(2,1)}), bf16[16,4,512]{2,1,0:T(4,128)(2,1)S(1)}, u32[]{:S(2)}, u32[]{:S(2)}) async-start(bf16[16,4,512]{2,1,0:T(4,128)(2,1)} %stack.2), calls=%async_computation | async-start | bytes 131072 | tf_op jit(solution)/shard_map/all_to_all | solution.py:92
  13.7 32.8 %all-gather = bf16[16,4,512]{2,1,0:T(4,128)(2,1)S(1)} all-gather(bf16[1,4,512]{2,1,0:T(4,128)(2,1)} %bitcast.138), channel_id=1, replica_groups=mesh['req'=16,'ctx'=16] {'ctx'}, dimensions={0}, use_global_device_ids=true | all-gather | bytes 69632 | tf_op jit(solution)/shard_map/all_gather | solution.py:89
  47.2 4.1 %reshape.243 = bf16[2048,4,128]{2,1,0:T(4,128)(2,1)} reshape(bf16[2048,512]{1,0:T(8,128)(2,1)} %param.12) | data formatting | bytes 4194304 | tf_op jit(solution)/shard_map/while/body/eval_jaxpr/reshape | solution.py:22
  51.3 2.0 reshape.244
  53.4 245.0 %while.24 = (s32[]{:T(128)}, bf16[4,8192]{1,0:T(4,128)(2,1)S(1)}, f32[4,8192]{1,0:T(4,128)S(1)}, f32[4,64]{1,0:T(4,128)S(1)}, f32[4,64]{1,0:T(4,128)S(1)}, /*ind...) while((s32[]{:T(128)}, bf16[4,8192]{1,0:T(4,128)(2,1)S(1)}, ...), condition=%wide.wide.region_4.5_spmd.clone.clone, body=%wide.wide.region_1.4_spmd.clone.clone.sunk | while | flops 273275904 | bytes 21383824 | solution.py:108
  55.0 2.5 fusion.68
  62.0 6.4 %collective-permute-done.2 = f32[4,64]{1,0:T(4,128)S(1)} collective-permute-done((f32[4,64]{1,0:T(4,128)S(1)}, f32[4,64]{1,0:T(4,128)S(1)}, u32[]{:S(2)}, u32[]{:S(2)}) %collective-permute-start.2) | collective-permute-done | bytes 1056 | tf_op jit(solution)/shard_map/while/body/eval_jaxpr/ppermute | solution.py:14
  70.1 2.5 fusion.68
  75.9 3.5 %collective-permute-start.3 = (f32[4,64]{1,0:T(4,128)S(1)}, f32[4,64]{1,0:T(4,128)S(1)}, u32[]{:S(2)}, u32[]{:S(2)}) collective-permute-start(f32[4,64]{1,0:T(4,128)S(1)} %get-tuple-element.509), channel_id=1, source_target_pairs={{0,1},{1,2},{2,3},{3,4},{4,5},{5,6},{6,7},{7,8},{8,9},{9,10},{10,1... | collective-permute-start | bytes 3080 | tf_op jit(solution)/shard_map/while/body/eval_jaxpr/ppermute | solution.py:14
  79.4 4.1 %collective-permute-done.2 = f32[4,64]{1,0:T(4,128)S(1)} collective-permute-done((f32[4,64]{1,0:T(4,128)S(1)}, f32[4,64]{1,0:T(4,128)S(1)}, u32[]{:S(2)}, u32[]{:S(2)}) %collective-permute-start.2) | collective-permute-done | bytes 1056 | tf_op jit(solution)/shard_map/while/body/eval_jaxpr/ppermute | solution.py:14
  85.1 2.5 fusion.68
  94.4 4.1 %collective-permute-done.2 = f32[4,64]{1,0:T(4,128)S(1)} collective-permute-done((f32[4,64]{1,0:T(4,128)S(1)}, f32[4,64]{1,0:T(4,128)S(1)}, u32[]{:S(2)}, u32[]{:S(2)}) %collective-permute-start.2) | collective-permute-done | bytes 1056 | tf_op jit(solution)/shard_map/while/body/eval_jaxpr/ppermute | solution.py:14
  100.1 2.5 fusion.68
  107.6 2.4 collective-permute-start.3
  110.0 3.8 %collective-permute-done.2 = f32[4,64]{1,0:T(4,128)S(1)} collective-permute-done((f32[4,64]{1,0:T(4,128)S(1)}, f32[4,64]{1,0:T(4,128)S(1)}, u32[]{:S(2)}, u32[]{:S(2)}) %collective-permute-start.2) | collective-permute-done | bytes 1056 | tf_op jit(solution)/shard_map/while/body/eval_jaxpr/ppermute | solution.py:14
  115.5 2.5 fusion.68
  122.6 3.0 collective-permute-start.3
  125.6 4.8 %collective-permute-done.2 = f32[4,64]{1,0:T(4,128)S(1)} collective-permute-done((f32[4,64]{1,0:T(4,128)S(1)}, f32[4,64]{1,0:T(4,128)S(1)}, u32[]{:S(2)}, u32[]{:S(2)}) %collective-permute-start.2) | collective-permute-done | bytes 1056 | tf_op jit(solution)/shard_map/while/body/eval_jaxpr/ppermute | solution.py:14
  132.0 2.5 fusion.68
  137.8 3.7 %collective-permute-start.3 = (f32[4,64]{1,0:T(4,128)S(1)}, f32[4,64]{1,0:T(4,128)S(1)}, u32[]{:S(2)}, u32[]{:S(2)}) collective-permute-start(f32[4,64]{1,0:T(4,128)S(1)} %get-tuple-element.509), channel_id=1, source_target_pairs={{0,1},{1,2},{2,3},{3,4},{4,5},{5,6},{6,7},{7,8},{8,9},{9,10},{10,1... | collective-permute-start | bytes 3080 | tf_op jit(solution)/shard_map/while/body/eval_jaxpr/ppermute | solution.py:14
  141.4 5.6 %collective-permute-done.2 = f32[4,64]{1,0:T(4,128)S(1)} collective-permute-done((f32[4,64]{1,0:T(4,128)S(1)}, f32[4,64]{1,0:T(4,128)S(1)}, u32[]{:S(2)}, u32[]{:S(2)}) %collective-permute-start.2) | collective-permute-done | bytes 1056 | tf_op jit(solution)/shard_map/while/body/eval_jaxpr/ppermute | solution.py:14
  148.7 2.5 fusion.68
  154.5 1.9 collective-permute-start.3
  156.4 6.5 %collective-permute-done.2 = f32[4,64]{1,0:T(4,128)S(1)} collective-permute-done((f32[4,64]{1,0:T(4,128)S(1)}, f32[4,64]{1,0:T(4,128)S(1)}, u32[]{:S(2)}, u32[]{:S(2)}) %collective-permute-start.2) | collective-permute-done | bytes 1056 | tf_op jit(solution)/shard_map/while/body/eval_jaxpr/ppermute | solution.py:14
  164.6 2.5 fusion.68
  170.4 2.7 collective-permute-start.3
  173.0 5.0 %collective-permute-done.2 = f32[4,64]{1,0:T(4,128)S(1)} collective-permute-done((f32[4,64]{1,0:T(4,128)S(1)}, f32[4,64]{1,0:T(4,128)S(1)}, u32[]{:S(2)}, u32[]{:S(2)}) %collective-permute-start.2) | collective-permute-done | bytes 1056 | tf_op jit(solution)/shard_map/while/body/eval_jaxpr/ppermute | solution.py:14
  179.6 2.5 fusion.68
  186.2 2.7 collective-permute-start.3
  188.9 4.1 %collective-permute-done.2 = f32[4,64]{1,0:T(4,128)S(1)} collective-permute-done((f32[4,64]{1,0:T(4,128)S(1)}, f32[4,64]{1,0:T(4,128)S(1)}, u32[]{:S(2)}, u32[]{:S(2)}) %collective-permute-start.2) | collective-permute-done | bytes 1056 | tf_op jit(solution)/shard_map/while/body/eval_jaxpr/ppermute | solution.py:14
  194.7 2.5 fusion.68
  204.0 4.1 %collective-permute-done.2 = f32[4,64]{1,0:T(4,128)S(1)} collective-permute-done((f32[4,64]{1,0:T(4,128)S(1)}, f32[4,64]{1,0:T(4,128)S(1)}, u32[]{:S(2)}, u32[]{:S(2)}) %collective-permute-start.2) | collective-permute-done | bytes 1056 | tf_op jit(solution)/shard_map/while/body/eval_jaxpr/ppermute | solution.py:14
  209.7 2.5 fusion.68
  219.0 4.1 %collective-permute-done.2 = f32[4,64]{1,0:T(4,128)S(1)} collective-permute-done((f32[4,64]{1,0:T(4,128)S(1)}, f32[4,64]{1,0:T(4,128)S(1)}, u32[]{:S(2)}, u32[]{:S(2)}) %collective-permute-start.2) | collective-permute-done | bytes 1056 | tf_op jit(solution)/shard_map/while/body/eval_jaxpr/ppermute | solution.py:14
  224.8 2.5 fusion.68
  232.2 1.9 collective-permute-start.3
  234.1 4.1 %collective-permute-done.2 = f32[4,64]{1,0:T(4,128)S(1)} collective-permute-done((f32[4,64]{1,0:T(4,128)S(1)}, f32[4,64]{1,0:T(4,128)S(1)}, u32[]{:S(2)}, u32[]{:S(2)}) %collective-permute-start.2) | collective-permute-done | bytes 1056 | tf_op jit(solution)/shard_map/while/body/eval_jaxpr/ppermute | solution.py:14
  239.8 2.5 fusion.68
  247.2 1.9 collective-permute-start.3
  249.1 4.1 %collective-permute-done.2 = f32[4,64]{1,0:T(4,128)S(1)} collective-permute-done((f32[4,64]{1,0:T(4,128)S(1)}, f32[4,64]{1,0:T(4,128)S(1)}, u32[]{:S(2)}, u32[]{:S(2)}) %collective-permute-start.2) | collective-permute-done | bytes 1056 | tf_op jit(solution)/shard_map/while/body/eval_jaxpr/ppermute | solution.py:14
  254.8 2.5 fusion.68
  262.2 1.9 collective-permute-start.3
  264.2 4.1 %collective-permute-done.2 = f32[4,64]{1,0:T(4,128)S(1)} collective-permute-done((f32[4,64]{1,0:T(4,128)S(1)}, f32[4,64]{1,0:T(4,128)S(1)}, u32[]{:S(2)}, u32[]{:S(2)}) %collective-permute-start.2) | collective-permute-done | bytes 1056 | tf_op jit(solution)/shard_map/while/body/eval_jaxpr/ppermute | solution.py:14
  269.9 2.5 fusion.68
  279.2 4.1 %collective-permute-done.2 = f32[4,64]{1,0:T(4,128)S(1)} collective-permute-done((f32[4,64]{1,0:T(4,128)S(1)}, f32[4,64]{1,0:T(4,128)S(1)}, u32[]{:S(2)}, u32[]{:S(2)}) %collective-permute-start.2) | collective-permute-done | bytes 1056 | tf_op jit(solution)/shard_map/while/body/eval_jaxpr/ppermute | solution.py:14
  284.9 2.5 fusion.68
  292.3 1.9 collective-permute-start.3
  294.3 4.1 %collective-permute-done.2 = f32[4,64]{1,0:T(4,128)S(1)} collective-permute-done((f32[4,64]{1,0:T(4,128)S(1)}, f32[4,64]{1,0:T(4,128)S(1)}, u32[]{:S(2)}, u32[]{:S(2)}) %collective-permute-start.2) | collective-permute-done | bytes 1056 | tf_op jit(solution)/shard_map/while/body/eval_jaxpr/ppermute | solution.py:14
  (419 shorter events, 97.1 us)
Async XLA Ops:
  2.2 296.6 %all-to-all-start = ((bf16[16,4,512]{2,1,0:T(4,128)(2,1)}), bf16[16,4,512]{2,1,0:T(4,128)(2,1)S(1)}, u32[]{:S(2)}, u32[]{:S(2)}) async-start(bf16[16,4,512]{2,1,0:T(4,128)(2,1)} %stack.2), calls=%async_computation | async-start | bytes 131072 | tf_op jit(solution)/shard_map/all_to_all | solution.py:92
  60.5 7.9 %collective-permute-start.1 = (f32[4,8192]{1,0:T(4,128)S(1)}, f32[4,8192]{1,0:T(4,128)S(1)}, u32[]{:S(2)}, u32[]{:S(2)}) collective-permute-start(f32[4,8192]{1,0:T(4,128)S(1)} %fusion.71), channel_id=1, source_target_pairs={{0,1},{1,2},{2,3},{3,4},{4,5},{5,6},{6,7},{7,8},{8,9},{9,10},{10,1... | collective-permute-start | bytes 393224 | tf_op jit(solution)/shard_map/while/body/eval_jaxpr/ppermute | solution.py:14
  60.6 7.8 %collective-permute-start = (bf16[4,8192]{1,0:T(4,128)(2,1)S(1)}, bf16[4,8192]{1,0:T(4,128)(2,1)S(1)}, u32[]{:S(2)}, u32[]{:S(2)}) collective-permute-start(bf16[4,8192]{1,0:T(4,128)(2,1)S(1)} %copy.160), channel_id=1, source_target_pairs={{0,1},{1,2},{2,3},{3,4},{4,5},{5,6},{6,7},{7,8},{8,9},{9,10},{10,1... | collective-permute-start | bytes 196616 | tf_op jit(solution)/shard_map/while/body/eval_jaxpr/ppermute | solution.py:14
  60.7 7.7 %collective-permute-start.2 = (f32[4,64]{1,0:T(4,128)S(1)}, f32[4,64]{1,0:T(4,128)S(1)}, u32[]{:S(2)}, u32[]{:S(2)}) collective-permute-start(f32[4,64]{1,0:T(4,128)S(1)} %get-tuple-element.508), channel_id=1, source_target_pairs={{0,1},{1,2},{2,3},{3,4},{4,5},{5,6},{6,7},{7,8},{8,9},{9,10},{10,1... | collective-permute-start | bytes 3080 | tf_op jit(solution)/shard_map/while/body/eval_jaxpr/ppermute | solution.py:14
  60.8 7.6 %collective-permute-start.3 = (f32[4,64]{1,0:T(4,128)S(1)}, f32[4,64]{1,0:T(4,128)S(1)}, u32[]{:S(2)}, u32[]{:S(2)}) collective-permute-start(f32[4,64]{1,0:T(4,128)S(1)} %get-tuple-element.509), channel_id=1, source_target_pairs={{0,1},{1,2},{2,3},{3,4},{4,5},{5,6},{6,7},{7,8},{8,9},{9,10},{10,1... | collective-permute-start | bytes 3080 | tf_op jit(solution)/shard_map/while/body/eval_jaxpr/ppermute | solution.py:14
  75.6 7.9 %collective-permute-start.1 = (f32[4,8192]{1,0:T(4,128)S(1)}, f32[4,8192]{1,0:T(4,128)S(1)}, u32[]{:S(2)}, u32[]{:S(2)}) collective-permute-start(f32[4,8192]{1,0:T(4,128)S(1)} %fusion.71), channel_id=1, source_target_pairs={{0,1},{1,2},{2,3},{3,4},{4,5},{5,6},{6,7},{7,8},{8,9},{9,10},{10,1... | collective-permute-start | bytes 393224 | tf_op jit(solution)/shard_map/while/body/eval_jaxpr/ppermute | solution.py:14
  75.7 7.8 %collective-permute-start = (bf16[4,8192]{1,0:T(4,128)(2,1)S(1)}, bf16[4,8192]{1,0:T(4,128)(2,1)S(1)}, u32[]{:S(2)}, u32[]{:S(2)}) collective-permute-start(bf16[4,8192]{1,0:T(4,128)(2,1)S(1)} %copy.160), channel_id=1, source_target_pairs={{0,1},{1,2},{2,3},{3,4},{4,5},{5,6},{6,7},{7,8},{8,9},{9,10},{10,1... | collective-permute-start | bytes 196616 | tf_op jit(solution)/shard_map/while/body/eval_jaxpr/ppermute | solution.py:14
  75.8 7.7 %collective-permute-start.2 = (f32[4,64]{1,0:T(4,128)S(1)}, f32[4,64]{1,0:T(4,128)S(1)}, u32[]{:S(2)}, u32[]{:S(2)}) collective-permute-start(f32[4,64]{1,0:T(4,128)S(1)} %get-tuple-element.508), channel_id=1, source_target_pairs={{0,1},{1,2},{2,3},{3,4},{4,5},{5,6},{6,7},{7,8},{8,9},{9,10},{10,1... | collective-permute-start | bytes 3080 | tf_op jit(solution)/shard_map/while/body/eval_jaxpr/ppermute | solution.py:14
  75.9 7.6 %collective-permute-start.3 = (f32[4,64]{1,0:T(4,128)S(1)}, f32[4,64]{1,0:T(4,128)S(1)}, u32[]{:S(2)}, u32[]{:S(2)}) collective-permute-start(f32[4,64]{1,0:T(4,128)S(1)} %get-tuple-element.509), channel_id=1, source_target_pairs={{0,1},{1,2},{2,3},{3,4},{4,5},{5,6},{6,7},{7,8},{8,9},{9,10},{10,1... | collective-permute-start | bytes 3080 | tf_op jit(solution)/shard_map/while/body/eval_jaxpr/ppermute | solution.py:14
  90.6 7.9 %collective-permute-start.1 = (f32[4,8192]{1,0:T(4,128)S(1)}, f32[4,8192]{1,0:T(4,128)S(1)}, u32[]{:S(2)}, u32[]{:S(2)}) collective-permute-start(f32[4,8192]{1,0:T(4,128)S(1)} %fusion.71), channel_id=1, source_target_pairs={{0,1},{1,2},{2,3},{3,4},{4,5},{5,6},{6,7},{7,8},{8,9},{9,10},{10,1... | collective-permute-start | bytes 393224 | tf_op jit(solution)/shard_map/while/body/eval_jaxpr/ppermute | solution.py:14
  90.7 7.8 %collective-permute-start = (bf16[4,8192]{1,0:T(4,128)(2,1)S(1)}, bf16[4,8192]{1,0:T(4,128)(2,1)S(1)}, u32[]{:S(2)}, u32[]{:S(2)}) collective-permute-start(bf16[4,8192]{1,0:T(4,128)(2,1)S(1)} %copy.160), channel_id=1, source_target_pairs={{0,1},{1,2},{2,3},{3,4},{4,5},{5,6},{6,7},{7,8},{8,9},{9,10},{10,1... | collective-permute-start | bytes 196616 | tf_op jit(solution)/shard_map/while/body/eval_jaxpr/ppermute | solution.py:14
  105.7 8.2 %collective-permute-start.1 = (f32[4,8192]{1,0:T(4,128)S(1)}, f32[4,8192]{1,0:T(4,128)S(1)}, u32[]{:S(2)}, u32[]{:S(2)}) collective-permute-start(f32[4,8192]{1,0:T(4,128)S(1)} %fusion.71), channel_id=1, source_target_pairs={{0,1},{1,2},{2,3},{3,4},{4,5},{5,6},{6,7},{7,8},{8,9},{9,10},{10,1... | collective-permute-start | bytes 393224 | tf_op jit(solution)/shard_map/while/body/eval_jaxpr/ppermute | solution.py:14
  105.8 8.1 %collective-permute-start = (bf16[4,8192]{1,0:T(4,128)(2,1)S(1)}, bf16[4,8192]{1,0:T(4,128)(2,1)S(1)}, u32[]{:S(2)}, u32[]{:S(2)}) collective-permute-start(bf16[4,8192]{1,0:T(4,128)(2,1)S(1)} %copy.160), channel_id=1, source_target_pairs={{0,1},{1,2},{2,3},{3,4},{4,5},{5,6},{6,7},{7,8},{8,9},{9,10},{10,1... | collective-permute-start | bytes 196616 | tf_op jit(solution)/shard_map/while/body/eval_jaxpr/ppermute | solution.py:14
  107.5 6.4 %collective-permute-start.2 = (f32[4,64]{1,0:T(4,128)S(1)}, f32[4,64]{1,0:T(4,128)S(1)}, u32[]{:S(2)}, u32[]{:S(2)}) collective-permute-start(f32[4,64]{1,0:T(4,128)S(1)} %get-tuple-element.508), channel_id=1, source_target_pairs={{0,1},{1,2},{2,3},{3,4},{4,5},{5,6},{6,7},{7,8},{8,9},{9,10},{10,1... | collective-permute-start | bytes 3080 | tf_op jit(solution)/shard_map/while/body/eval_jaxpr/ppermute | solution.py:14
  121.0 9.4 %collective-permute-start.1 = (f32[4,8192]{1,0:T(4,128)S(1)}, f32[4,8192]{1,0:T(4,128)S(1)}, u32[]{:S(2)}, u32[]{:S(2)}) collective-permute-start(f32[4,8192]{1,0:T(4,128)S(1)} %fusion.71), channel_id=1, source_target_pairs={{0,1},{1,2},{2,3},{3,4},{4,5},{5,6},{6,7},{7,8},{8,9},{9,10},{10,1... | collective-permute-start | bytes 393224 | tf_op jit(solution)/shard_map/while/body/eval_jaxpr/ppermute | solution.py:14
  121.1 9.3 %collective-permute-start = (bf16[4,8192]{1,0:T(4,128)(2,1)S(1)}, bf16[4,8192]{1,0:T(4,128)(2,1)S(1)}, u32[]{:S(2)}, u32[]{:S(2)}) collective-permute-start(bf16[4,8192]{1,0:T(4,128)(2,1)S(1)} %copy.160), channel_id=1, source_target_pairs={{0,1},{1,2},{2,3},{3,4},{4,5},{5,6},{6,7},{7,8},{8,9},{9,10},{10,1... | collective-permute-start | bytes 196616 | tf_op jit(solution)/shard_map/while/body/eval_jaxpr/ppermute | solution.py:14
  122.5 7.8 %collective-permute-start.2 = (f32[4,64]{1,0:T(4,128)S(1)}, f32[4,64]{1,0:T(4,128)S(1)}, u32[]{:S(2)}, u32[]{:S(2)}) collective-permute-start(f32[4,64]{1,0:T(4,128)S(1)} %get-tuple-element.508), channel_id=1, source_target_pairs={{0,1},{1,2},{2,3},{3,4},{4,5},{5,6},{6,7},{7,8},{8,9},{9,10},{10,1... | collective-permute-start | bytes 3080 | tf_op jit(solution)/shard_map/while/body/eval_jaxpr/ppermute | solution.py:14
  122.6 7.8 %collective-permute-start.3 = (f32[4,64]{1,0:T(4,128)S(1)}, f32[4,64]{1,0:T(4,128)S(1)}, u32[]{:S(2)}, u32[]{:S(2)}) collective-permute-start(f32[4,64]{1,0:T(4,128)S(1)} %get-tuple-element.509), channel_id=1, source_target_pairs={{0,1},{1,2},{2,3},{3,4},{4,5},{5,6},{6,7},{7,8},{8,9},{9,10},{10,1... | collective-permute-start | bytes 3080 | tf_op jit(solution)/shard_map/while/body/eval_jaxpr/ppermute | solution.py:14
  137.5 9.6 %collective-permute-start.1 = (f32[4,8192]{1,0:T(4,128)S(1)}, f32[4,8192]{1,0:T(4,128)S(1)}, u32[]{:S(2)}, u32[]{:S(2)}) collective-permute-start(f32[4,8192]{1,0:T(4,128)S(1)} %fusion.71), channel_id=1, source_target_pairs={{0,1},{1,2},{2,3},{3,4},{4,5},{5,6},{6,7},{7,8},{8,9},{9,10},{10,1... | collective-permute-start | bytes 393224 | tf_op jit(solution)/shard_map/while/body/eval_jaxpr/ppermute | solution.py:14
  137.6 9.5 %collective-permute-start = (bf16[4,8192]{1,0:T(4,128)(2,1)S(1)}, bf16[4,8192]{1,0:T(4,128)(2,1)S(1)}, u32[]{:S(2)}, u32[]{:S(2)}) collective-permute-start(bf16[4,8192]{1,0:T(4,128)(2,1)S(1)} %copy.160), channel_id=1, source_target_pairs={{0,1},{1,2},{2,3},{3,4},{4,5},{5,6},{6,7},{7,8},{8,9},{9,10},{10,1... | collective-permute-start | bytes 196616 | tf_op jit(solution)/shard_map/while/body/eval_jaxpr/ppermute | solution.py:14
  137.7 9.4 %collective-permute-start.2 = (f32[4,64]{1,0:T(4,128)S(1)}, f32[4,64]{1,0:T(4,128)S(1)}, u32[]{:S(2)}, u32[]{:S(2)}) collective-permute-start(f32[4,64]{1,0:T(4,128)S(1)} %get-tuple-element.508), channel_id=1, source_target_pairs={{0,1},{1,2},{2,3},{3,4},{4,5},{5,6},{6,7},{7,8},{8,9},{9,10},{10,1... | collective-permute-start | bytes 3080 | tf_op jit(solution)/shard_map/while/body/eval_jaxpr/ppermute | solution.py:14
  137.8 9.3 %collective-permute-start.3 = (f32[4,64]{1,0:T(4,128)S(1)}, f32[4,64]{1,0:T(4,128)S(1)}, u32[]{:S(2)}, u32[]{:S(2)}) collective-permute-start(f32[4,64]{1,0:T(4,128)S(1)} %get-tuple-element.509), channel_id=1, source_target_pairs={{0,1},{1,2},{2,3},{3,4},{4,5},{5,6},{6,7},{7,8},{8,9},{9,10},{10,1... | collective-permute-start | bytes 3080 | tf_op jit(solution)/shard_map/while/body/eval_jaxpr/ppermute | solution.py:14
  154.3 8.7 %collective-permute-start.1 = (f32[4,8192]{1,0:T(4,128)S(1)}, f32[4,8192]{1,0:T(4,128)S(1)}, u32[]{:S(2)}, u32[]{:S(2)}) collective-permute-start(f32[4,8192]{1,0:T(4,128)S(1)} %fusion.71), channel_id=1, source_target_pairs={{0,1},{1,2},{2,3},{3,4},{4,5},{5,6},{6,7},{7,8},{8,9},{9,10},{10,1... | collective-permute-start | bytes 393224 | tf_op jit(solution)/shard_map/while/body/eval_jaxpr/ppermute | solution.py:14
  154.3 8.6 %collective-permute-start = (bf16[4,8192]{1,0:T(4,128)(2,1)S(1)}, bf16[4,8192]{1,0:T(4,128)(2,1)S(1)}, u32[]{:S(2)}, u32[]{:S(2)}) collective-permute-start(bf16[4,8192]{1,0:T(4,128)(2,1)S(1)} %copy.160), channel_id=1, source_target_pairs={{0,1},{1,2},{2,3},{3,4},{4,5},{5,6},{6,7},{7,8},{8,9},{9,10},{10,1... | collective-permute-start | bytes 196616 | tf_op jit(solution)/shard_map/while/body/eval_jaxpr/ppermute | solution.py:14
  154.4 8.5 %collective-permute-start.2 = (f32[4,64]{1,0:T(4,128)S(1)}, f32[4,64]{1,0:T(4,128)S(1)}, u32[]{:S(2)}, u32[]{:S(2)}) collective-permute-start(f32[4,64]{1,0:T(4,128)S(1)} %get-tuple-element.508), channel_id=1, source_target_pairs={{0,1},{1,2},{2,3},{3,4},{4,5},{5,6},{6,7},{7,8},{8,9},{9,10},{10,1... | collective-permute-start | bytes 3080 | tf_op jit(solution)/shard_map/while/body/eval_jaxpr/ppermute | solution.py:14
  154.5 8.4 %collective-permute-start.3 = (f32[4,64]{1,0:T(4,128)S(1)}, f32[4,64]{1,0:T(4,128)S(1)}, u32[]{:S(2)}, u32[]{:S(2)}) collective-permute-start(f32[4,64]{1,0:T(4,128)S(1)} %get-tuple-element.509), channel_id=1, source_target_pairs={{0,1},{1,2},{2,3},{3,4},{4,5},{5,6},{6,7},{7,8},{8,9},{9,10},{10,1... | collective-permute-start | bytes 3080 | tf_op jit(solution)/shard_map/while/body/eval_jaxpr/ppermute | solution.py:14
  170.1 7.9 %collective-permute-start.1 = (f32[4,8192]{1,0:T(4,128)S(1)}, f32[4,8192]{1,0:T(4,128)S(1)}, u32[]{:S(2)}, u32[]{:S(2)}) collective-permute-start(f32[4,8192]{1,0:T(4,128)S(1)} %fusion.71), channel_id=1, source_target_pairs={{0,1},{1,2},{2,3},{3,4},{4,5},{5,6},{6,7},{7,8},{8,9},{9,10},{10,1... | collective-permute-start | bytes 393224 | tf_op jit(solution)/shard_map/while/body/eval_jaxpr/ppermute | solution.py:14
  170.2 7.8 %collective-permute-start = (bf16[4,8192]{1,0:T(4,128)(2,1)S(1)}, bf16[4,8192]{1,0:T(4,128)(2,1)S(1)}, u32[]{:S(2)}, u32[]{:S(2)}) collective-permute-start(bf16[4,8192]{1,0:T(4,128)(2,1)S(1)} %copy.160), channel_id=1, source_target_pairs={{0,1},{1,2},{2,3},{3,4},{4,5},{5,6},{6,7},{7,8},{8,9},{9,10},{10,1... | collective-permute-start | bytes 196616 | tf_op jit(solution)/shard_map/while/body/eval_jaxpr/ppermute | solution.py:14
  170.3 7.7 %collective-permute-start.2 = (f32[4,64]{1,0:T(4,128)S(1)}, f32[4,64]{1,0:T(4,128)S(1)}, u32[]{:S(2)}, u32[]{:S(2)}) collective-permute-start(f32[4,64]{1,0:T(4,128)S(1)} %get-tuple-element.508), channel_id=1, source_target_pairs={{0,1},{1,2},{2,3},{3,4},{4,5},{5,6},{6,7},{7,8},{8,9},{9,10},{10,1... | collective-permute-start | bytes 3080 | tf_op jit(solution)/shard_map/while/body/eval_jaxpr/ppermute | solution.py:14
  170.4 7.6 %collective-permute-start.3 = (f32[4,64]{1,0:T(4,128)S(1)}, f32[4,64]{1,0:T(4,128)S(1)}, u32[]{:S(2)}, u32[]{:S(2)}) collective-permute-start(f32[4,64]{1,0:T(4,128)S(1)} %get-tuple-element.509), channel_id=1, source_target_pairs={{0,1},{1,2},{2,3},{3,4},{4,5},{5,6},{6,7},{7,8},{8,9},{9,10},{10,1... | collective-permute-start | bytes 3080 | tf_op jit(solution)/shard_map/while/body/eval_jaxpr/ppermute | solution.py:14
  185.2 7.9 %collective-permute-start.1 = (f32[4,8192]{1,0:T(4,128)S(1)}, f32[4,8192]{1,0:T(4,128)S(1)}, u32[]{:S(2)}, u32[]{:S(2)}) collective-permute-start(f32[4,8192]{1,0:T(4,128)S(1)} %fusion.71), channel_id=1, source_target_pairs={{0,1},{1,2},{2,3},{3,4},{4,5},{5,6},{6,7},{7,8},{8,9},{9,10},{10,1... | collective-permute-start | bytes 393224 | tf_op jit(solution)/shard_map/while/body/eval_jaxpr/ppermute | solution.py:14
  185.2 7.8 %collective-permute-start = (bf16[4,8192]{1,0:T(4,128)(2,1)S(1)}, bf16[4,8192]{1,0:T(4,128)(2,1)S(1)}, u32[]{:S(2)}, u32[]{:S(2)}) collective-permute-start(bf16[4,8192]{1,0:T(4,128)(2,1)S(1)} %copy.160), channel_id=1, source_target_pairs={{0,1},{1,2},{2,3},{3,4},{4,5},{5,6},{6,7},{7,8},{8,9},{9,10},{10,1... | collective-permute-start | bytes 196616 | tf_op jit(solution)/shard_map/while/body/eval_jaxpr/ppermute | solution.py:14
  186.1 6.9 %collective-permute-start.2 = (f32[4,64]{1,0:T(4,128)S(1)}, f32[4,64]{1,0:T(4,128)S(1)}, u32[]{:S(2)}, u32[]{:S(2)}) collective-permute-start(f32[4,64]{1,0:T(4,128)S(1)} %get-tuple-element.508), channel_id=1, source_target_pairs={{0,1},{1,2},{2,3},{3,4},{4,5},{5,6},{6,7},{7,8},{8,9},{9,10},{10,1... | collective-permute-start | bytes 3080 | tf_op jit(solution)/shard_map/while/body/eval_jaxpr/ppermute | solution.py:14
  186.2 6.9 %collective-permute-start.3 = (f32[4,64]{1,0:T(4,128)S(1)}, f32[4,64]{1,0:T(4,128)S(1)}, u32[]{:S(2)}, u32[]{:S(2)}) collective-permute-start(f32[4,64]{1,0:T(4,128)S(1)} %get-tuple-element.509), channel_id=1, source_target_pairs={{0,1},{1,2},{2,3},{3,4},{4,5},{5,6},{6,7},{7,8},{8,9},{9,10},{10,1... | collective-permute-start | bytes 3080 | tf_op jit(solution)/shard_map/while/body/eval_jaxpr/ppermute | solution.py:14
  200.2 7.9 %collective-permute-start.1 = (f32[4,8192]{1,0:T(4,128)S(1)}, f32[4,8192]{1,0:T(4,128)S(1)}, u32[]{:S(2)}, u32[]{:S(2)}) collective-permute-start(f32[4,8192]{1,0:T(4,128)S(1)} %fusion.71), channel_id=1, source_target_pairs={{0,1},{1,2},{2,3},{3,4},{4,5},{5,6},{6,7},{7,8},{8,9},{9,10},{10,1... | collective-permute-start | bytes 393224 | tf_op jit(solution)/shard_map/while/body/eval_jaxpr/ppermute | solution.py:14
  200.3 7.8 %collective-permute-start = (bf16[4,8192]{1,0:T(4,128)(2,1)S(1)}, bf16[4,8192]{1,0:T(4,128)(2,1)S(1)}, u32[]{:S(2)}, u32[]{:S(2)}) collective-permute-start(bf16[4,8192]{1,0:T(4,128)(2,1)S(1)} %copy.160), channel_id=1, source_target_pairs={{0,1},{1,2},{2,3},{3,4},{4,5},{5,6},{6,7},{7,8},{8,9},{9,10},{10,1... | collective-permute-start | bytes 196616 | tf_op jit(solution)/shard_map/while/body/eval_jaxpr/ppermute | solution.py:14
  215.2 7.9 %collective-permute-start.1 = (f32[4,8192]{1,0:T(4,128)S(1)}, f32[4,8192]{1,0:T(4,128)S(1)}, u32[]{:S(2)}, u32[]{:S(2)}) collective-permute-start(f32[4,8192]{1,0:T(4,128)S(1)} %fusion.71), channel_id=1, source_target_pairs={{0,1},{1,2},{2,3},{3,4},{4,5},{5,6},{6,7},{7,8},{8,9},{9,10},{10,1... | collective-permute-start | bytes 393224 | tf_op jit(solution)/shard_map/while/body/eval_jaxpr/ppermute | solution.py:14
  215.3 7.8 %collective-permute-start = (bf16[4,8192]{1,0:T(4,128)(2,1)S(1)}, bf16[4,8192]{1,0:T(4,128)(2,1)S(1)}, u32[]{:S(2)}, u32[]{:S(2)}) collective-permute-start(bf16[4,8192]{1,0:T(4,128)(2,1)S(1)} %copy.160), channel_id=1, source_target_pairs={{0,1},{1,2},{2,3},{3,4},{4,5},{5,6},{6,7},{7,8},{8,9},{9,10},{10,1... | collective-permute-start | bytes 196616 | tf_op jit(solution)/shard_map/while/body/eval_jaxpr/ppermute | solution.py:14
  230.3 7.9 %collective-permute-start.1 = (f32[4,8192]{1,0:T(4,128)S(1)}, f32[4,8192]{1,0:T(4,128)S(1)}, u32[]{:S(2)}, u32[]{:S(2)}) collective-permute-start(f32[4,8192]{1,0:T(4,128)S(1)} %fusion.71), channel_id=1, source_target_pairs={{0,1},{1,2},{2,3},{3,4},{4,5},{5,6},{6,7},{7,8},{8,9},{9,10},{10,1... | collective-permute-start | bytes 393224 | tf_op jit(solution)/shard_map/while/body/eval_jaxpr/ppermute | solution.py:14
  230.4 7.8 %collective-permute-start = (bf16[4,8192]{1,0:T(4,128)(2,1)S(1)}, bf16[4,8192]{1,0:T(4,128)(2,1)S(1)}, u32[]{:S(2)}, u32[]{:S(2)}) collective-permute-start(bf16[4,8192]{1,0:T(4,128)(2,1)S(1)} %copy.160), channel_id=1, source_target_pairs={{0,1},{1,2},{2,3},{3,4},{4,5},{5,6},{6,7},{7,8},{8,9},{9,10},{10,1... | collective-permute-start | bytes 196616 | tf_op jit(solution)/shard_map/while/body/eval_jaxpr/ppermute | solution.py:14
  245.3 7.9 %collective-permute-start.1 = (f32[4,8192]{1,0:T(4,128)S(1)}, f32[4,8192]{1,0:T(4,128)S(1)}, u32[]{:S(2)}, u32[]{:S(2)}) collective-permute-start(f32[4,8192]{1,0:T(4,128)S(1)} %fusion.71), channel_id=1, source_target_pairs={{0,1},{1,2},{2,3},{3,4},{4,5},{5,6},{6,7},{7,8},{8,9},{9,10},{10,1... | collective-permute-start | bytes 393224 | tf_op jit(solution)/shard_map/while/body/eval_jaxpr/ppermute | solution.py:14
  245.4 7.8 %collective-permute-start = (bf16[4,8192]{1,0:T(4,128)(2,1)S(1)}, bf16[4,8192]{1,0:T(4,128)(2,1)S(1)}, u32[]{:S(2)}, u32[]{:S(2)}) collective-permute-start(bf16[4,8192]{1,0:T(4,128)(2,1)S(1)} %copy.160), channel_id=1, source_target_pairs={{0,1},{1,2},{2,3},{3,4},{4,5},{5,6},{6,7},{7,8},{8,9},{9,10},{10,1... | collective-permute-start | bytes 196616 | tf_op jit(solution)/shard_map/while/body/eval_jaxpr/ppermute | solution.py:14
  260.4 7.9 %collective-permute-start.1 = (f32[4,8192]{1,0:T(4,128)S(1)}, f32[4,8192]{1,0:T(4,128)S(1)}, u32[]{:S(2)}, u32[]{:S(2)}) collective-permute-start(f32[4,8192]{1,0:T(4,128)S(1)} %fusion.71), channel_id=1, source_target_pairs={{0,1},{1,2},{2,3},{3,4},{4,5},{5,6},{6,7},{7,8},{8,9},{9,10},{10,1... | collective-permute-start | bytes 393224 | tf_op jit(solution)/shard_map/while/body/eval_jaxpr/ppermute | solution.py:14
  260.4 7.8 %collective-permute-start = (bf16[4,8192]{1,0:T(4,128)(2,1)S(1)}, bf16[4,8192]{1,0:T(4,128)(2,1)S(1)}, u32[]{:S(2)}, u32[]{:S(2)}) collective-permute-start(bf16[4,8192]{1,0:T(4,128)(2,1)S(1)} %copy.160), channel_id=1, source_target_pairs={{0,1},{1,2},{2,3},{3,4},{4,5},{5,6},{6,7},{7,8},{8,9},{9,10},{10,1... | collective-permute-start | bytes 196616 | tf_op jit(solution)/shard_map/while/body/eval_jaxpr/ppermute | solution.py:14
  275.4 7.9 %collective-permute-start.1 = (f32[4,8192]{1,0:T(4,128)S(1)}, f32[4,8192]{1,0:T(4,128)S(1)}, u32[]{:S(2)}, u32[]{:S(2)}) collective-permute-start(f32[4,8192]{1,0:T(4,128)S(1)} %fusion.71), channel_id=1, source_target_pairs={{0,1},{1,2},{2,3},{3,4},{4,5},{5,6},{6,7},{7,8},{8,9},{9,10},{10,1... | collective-permute-start | bytes 393224 | tf_op jit(solution)/shard_map/while/body/eval_jaxpr/ppermute | solution.py:14
  275.5 7.8 %collective-permute-start = (bf16[4,8192]{1,0:T(4,128)(2,1)S(1)}, bf16[4,8192]{1,0:T(4,128)(2,1)S(1)}, u32[]{:S(2)}, u32[]{:S(2)}) collective-permute-start(bf16[4,8192]{1,0:T(4,128)(2,1)S(1)} %copy.160), channel_id=1, source_target_pairs={{0,1},{1,2},{2,3},{3,4},{4,5},{5,6},{6,7},{7,8},{8,9},{9,10},{10,1... | collective-permute-start | bytes 196616 | tf_op jit(solution)/shard_map/while/body/eval_jaxpr/ppermute | solution.py:14
  290.4 7.9 %collective-permute-start.1 = (f32[4,8192]{1,0:T(4,128)S(1)}, f32[4,8192]{1,0:T(4,128)S(1)}, u32[]{:S(2)}, u32[]{:S(2)}) collective-permute-start(f32[4,8192]{1,0:T(4,128)S(1)} %fusion.71), channel_id=1, source_target_pairs={{0,1},{1,2},{2,3},{3,4},{4,5},{5,6},{6,7},{7,8},{8,9},{9,10},{10,1... | collective-permute-start | bytes 393224 | tf_op jit(solution)/shard_map/while/body/eval_jaxpr/ppermute | solution.py:14
  290.5 7.8 %collective-permute-start = (bf16[4,8192]{1,0:T(4,128)(2,1)S(1)}, bf16[4,8192]{1,0:T(4,128)(2,1)S(1)}, u32[]{:S(2)}, u32[]{:S(2)}) collective-permute-start(bf16[4,8192]{1,0:T(4,128)(2,1)S(1)} %copy.160), channel_id=1, source_target_pairs={{0,1},{1,2},{2,3},{3,4},{4,5},{5,6},{6,7},{7,8},{8,9},{9,10},{10,1... | collective-permute-start | bytes 196616 | tf_op jit(solution)/shard_map/while/body/eval_jaxpr/ppermute | solution.py:14
  (34 other events, 132.7 us)
